TPU v7x, 32 devices: a whole 2x2x4 slice. The times are simulated.
32 devices in a mesh: sample: 4 (over y, x), seq: 4 (over z), head: 2 (over core).
Axes of the slice: x: 2, y: 2, z: 4, core: 2. Of those that a mesh axis runs over, the one named last changes fastest.
Arguments:
- values: bfloat16 [4, 2048, 4096], P('sample', 'seq', 'head'), may hold values from -6 to 6
- gate_values: bfloat16 [4, 2048, 4096], P('sample', 'seq', 'head'), may hold values from -6 to 6
- state_in: bfloat16 [4, 2048, 128], P('sample', 'seq'), may hold values from -0.5 to 0.5
- state_out: bfloat16 [4, 2048, 128], P('sample', 'seq'), may hold values from -0.5 to 0.5
- step_size: float32 [4, 2048, 64], P('sample', 'seq', 'head'), may hold values from 0.25 to 1
- log_decay: float32 [4, 2048, 64], P('sample', 'seq', 'head'), may hold values from -1 to 0, as said below
- skip_gain: float32 [64], P('head'), may hold values from 0.5 to 1.5
- norm_gain: float32 [4096], P('head'), may hold values from 0.25 to 1.75
- out_weight: bfloat16 [4096, 4096], P('head', 'seq'), may hold values from -0.09375 to 0.09375
- prompt_state: float32 [64, 64, 128], P('head', None, 'sample'), may hold values from -16 to 16
Outputs:
- projected: bfloat16 [4, 2048, 4096], P('sample', 'seq', 'head')
Inputs may be any that keep to these rules, and one draw needn't show every extreme that they name: `log_decay`: every entry is negative.
All inputs are finite; a program needn't handle non-finite values.
Results may differ from a plain program's by a relative error of at most 0.019.
Values may be sent and summed in bfloat16 or wider, within the bound.
No kernel may reach another device: no remote copies, remote signals or barrier semaphores. Data moves between devices by JAX's collectives and lax.ppermute only.
A program may use at most 128 MiB of HBM per device.

v0:
```python
from functools import partial
import jax
import jax.numpy as jnp
from jax import lax
from jax.sharding import PartitionSpec as P

P_SIZE = 64
L = 256
GROUP_HEADS = 8
EPSILON = 1e-05


def carried_in(array, axis, join, neutral):
    place = lax.axis_index(axis)
    gathered = jax.tree.map(
        lambda a, kind: lax.all_gather(a.astype(kind), axis), array, (jnp.bfloat16, jnp.bfloat16)
    )
    state = jax.tree.map(lambda a, e: jnp.zeros_like(a) + jnp.asarray(e, a.dtype), array, neutral)

    def one(step, state):
        return join(
            state,
            jax.tree.map(
                lambda a, own: lax.dynamic_index_in_dim(a, step, 0, False).astype(own.dtype),
                gathered,
                array,
            ),
        )

    return lax.fori_loop(0, place, one, state)


def block_terms(values_blk, in_blk, out_blk, step_blk, decay_blk, skip_gain):
    heads = decay_blk.shape[1]
    running = jnp.cumsum(decay_blk, axis=0)
    per_head = values_blk.reshape(values_blk.shape[0], heads, -1)
    scaled = (per_head.astype(jnp.float32) * step_blk[:, :, None]).astype(jnp.bfloat16)
    scores = jnp.dot(out_blk, in_blk.T, preferred_element_type=jnp.float32)
    token_offset = jnp.arange(values_blk.shape[0])
    causal = token_offset[:, None] >= token_offset[None, :]
    by_head = running.T
    spread = by_head[:, :, None] - by_head[:, None, :]
    pair_decay = jnp.exp(jnp.where(causal[None], spread, -1e30))
    mixing = (scores[None] * pair_decay).astype(jnp.bfloat16)
    inner = jnp.einsum("hts,shp->thp", mixing, scaled, preferred_element_type=jnp.float32)
    tail = jnp.exp(running[-1][None, :] - running)
    weighted = (scaled.astype(jnp.float32) * tail[:, :, None]).astype(jnp.bfloat16)
    block_state = jnp.einsum("shp,sn->hpn", weighted, in_blk, preferred_element_type=jnp.float32)
    local_out = inner + skip_gain[None, :, None] * per_head.astype(jnp.float32)
    return (local_out, running, block_state)


def local_sweep(values_s, in_s, out_s, step_s, decay_s, skip_gain):
    count = values_s.shape[0] // L
    heads = decay_s.shape[1]
    width = values_s.shape[1] // heads
    states = in_s.shape[1]
    blocks = (
        values_s.reshape(count, L, -1),
        in_s.reshape(count, L, -1),
        out_s.reshape(count, L, -1),
        step_s.reshape(count, L, heads),
        decay_s.reshape(count, L, heads),
    )

    def advance(carry, block):
        state, total = carry
        values_blk, in_blk, out_blk, step_blk, decay_blk = block
        local_out, running, block_state = block_terms(
            values_blk, in_blk, out_blk, step_blk, decay_blk, skip_gain
        )
        new_state = jnp.exp(running[-1])[:, None, None] * state + block_state
        return ((new_state, total + running[-1]), (local_out, running, state, total))

    initial = (jnp.zeros((heads, width, states), jnp.float32), jnp.zeros((heads,), jnp.float32))
    return lax.scan(advance, initial, blocks)


def link(earlier, later):
    decay_early, state_early = earlier
    decay_late, state_late = later
    return (decay_early * decay_late, decay_late[:, :, None, None] * state_early + state_late)


def group_norm(gated, norm_gain):
    width = GROUP_HEADS * P_SIZE
    grouped = gated.reshape(gated.shape[0], -1, width)
    mean_square = jnp.mean(grouped * grouped, axis=-1, keepdims=True)
    rescaled = grouped * lax.rsqrt(mean_square + EPSILON)
    return (rescaled.reshape(gated.shape) * norm_gain).astype(jnp.bfloat16)


def shards(
    values,
    gate_values,
    state_in,
    state_out,
    step_size,
    log_decay,
    skip_gain,
    norm_gain,
    out_weight,
    prompt_state,
):
    prompt = lax.all_gather(prompt_state.astype(jnp.bfloat16), "sample", axis=2, tiled=True).astype(
        prompt_state.dtype
    )
    sweep_sample = partial(local_sweep, skip_gain=skip_gain)
    (last_state, last_total), (local_out, running, before, totals) = jax.vmap(sweep_sample)(
        values, state_in, state_out, step_size, log_decay
    )
    identity = (jnp.ones_like(last_total), jnp.zeros_like(last_state))
    lead_decay, lead_state = carried_in((jnp.exp(last_total), last_state), "seq", link, identity)
    entry = lead_state + lead_decay[:, :, None, None] * prompt[None]
    start = before + jnp.exp(totals)[:, :, :, None, None] * entry[:, None]
    start_low = start.astype(jnp.bfloat16)
    samples, tokens = (values.shape[0], values.shape[1])
    count = tokens // L
    out_blocks = state_out.reshape(samples, count, L, -1)
    carried = jnp.exp(running)[..., None] * jnp.einsum(
        "sktn,skhpn->skthp", out_blocks, start_low, preferred_element_type=jnp.float32
    )
    outputs = (local_out + carried).reshape(samples * tokens, -1)
    gated = outputs * jax.nn.silu(gate_values.reshape(samples * tokens, -1).astype(jnp.float32))
    normed = group_norm(gated, norm_gain)
    terms = jnp.dot(
        normed,
        lax.all_gather(out_weight, "seq", axis=1, tiled=True),
        preferred_element_type=jnp.float32,
    )
    mine = lax.psum_scatter(terms.astype(jnp.bfloat16), "head", scatter_dimension=1, tiled=True)
    return mine.reshape(samples, tokens, -1)


def solution(mesh):
    in_specs = (
        P("sample", "seq", "head"),
        P("sample", "seq", "head"),
        P("sample", "seq", None),
        P("sample", "seq", None),
        P("sample", "seq", "head"),
        P("sample", "seq", "head"),
        P("head"),
        P("head"),
        P("head", "seq"),
        P("head", None, "sample"),
    )
    out_specs = P("sample", "seq", "head")
    return jax.shard_map(shards, mesh=mesh, in_specs=in_specs, out_specs=out_specs, check_vma=False)
```

profile of v0, /device:TPU:0, one launch (start us, length us, event | category | flops | bytes accessed | tf_op | source)
XLA Modules:
  0.0 398.6 jit_solution(10033825159931947701)
XLA Ops:
  6.5 0.9 reshape.287
  7.4 0.9 reshape.289
  8.3 22.4 %while.34 = (s32[]{:T(128)}, f32[1,32,64,128]{3,2,1,0:T(8,128)S(1)}, f32[1,32]{1,0:T(1,128)S(1)}, f32[2,1,256,32,64]{2,4,3,1,0:T(8,128)}, f32[2,1,256,32]{2,0,3,...) while((s32[]{:T(128)}, ...), condition=%wide.region_3.4_spmd.clone, body=%wide.region_0.3_spmd.clone.sunk | while | flops 435765440 | bytes 33923384 | solution.py:76
  8.5 0.6 reduce-window.14
  9.6 1.3 constant_dynamic-slice_fusion.7
  10.9 0.5 copy.91
  11.8 3.7 fusion.49
  17.1 1.0 bitcast_dynamic-update-slice_fusion.2
  18.9 0.6 copy-done.9
  19.6 0.6 reduce-window.14
  20.7 1.3 constant_dynamic-slice_fusion.7
  22.0 0.5 copy.91
  23.0 3.8 fusion.49
  28.3 1.0 bitcast_dynamic-update-slice_fusion.2
  30.0 0.6 copy-done.9
  30.7 0.9 convert_element_type.137
  31.6 0.7 all-gather.6.cloned.1.call-update
  32.8 2.9 copy.55
  35.7 4.0 reshape.301
  39.7 12.9 %all-gather.2 = bf16[4,1,32]{2,1,0:T(2,128)(2,1)S(1)} all-gather(bf16[1,1,32]{2,1,0:T(2,128)(2,1)S(1)} %convert_bitcast_fusion.1), channel_id=2, replica_groups=mesh['sample'=4,'seq'=4,'head'=2] {'seq'}, dimensions={0}, use_global_device_ids=true | all-gather | bytes 320 | tf_op jit(solution)/shard_map/all_gather | solution.py:16
  52.6 13.7 %all_gather.22 = bf16[32,64,128]{1,0,2:T(8,128)(2,1)} all-gather(bf16[32,64,32]{1,0,2:T(8,128)(2,1)S(1)} %copy.72), channel_id=1, replica_groups=mesh['sample'=4,'seq'=4,'head'=2] {'sample'}, dimensions={2}, use_global_device_ids=true | all-gather | bytes 655360 | tf_op jit(solution)/shard_map/all_gather | solution.py:105
  66.3 13.9 %all-gather.8.cloned.1.call-done = bf16[4,32,64,128]{3,2,1,0:T(8,128)(2,1)} async-done(((bf16[1,32,64,128]{3,2,1,0:T(8,128)(2,1)}), bf16[4,32,64,128]{3,2,1,0:T(8,128)(2,1)}) %all-gather.8.cloned.1.call-update) | async-done | bytes 2097168 | tf_op jit(solution)/shard_map/all_gather | solution.py:16
  80.3 2.8 copy.52
  83.1 3.6 fusion.27
  86.8 3.0 copy.53
  89.8 6.7 %multiply_reduce_fusion = (f32[2,256,32]{1,2,0:T(8,128)S(1)}, f32[2,256,32,64]{1,3,2,0:T(8,128)S(1)}) fusion(f32[2,256,32,64]{1,0,3,2:T(2,128)} %reshape.301, bf16[2,256,128,1]{2,1,3,0:T(8,128)(2,1)S(1)} %bitcast.226, f32[2,1,32,64,128]{4,3,2,1,0:T(8,128)} %get-tuple-element.113, f32[32,64,128]{2,1,0:T(8,128)S(1)} %copy.53, f32[2,32]{1,0:T(2,128)S(1)} %bitcast.229, ...), kind=kOutput, calls=%fused_computation.59 | convolution fusion | flops 279429120 | bytes 15991040 | tf_op jit(solution)/shard_map/sktn,skhpn->skthp/dot_general | solution.py:120
  96.6 3.4 copy.54
  99.9 2.4 copy.65
  102.5 4.0 %fusion.21 = bf16[512,2048]{0,1:T(8,128)(2,1)} fusion(f32[512,2048]{0,1:T(8,128)} %bitcast.212, f32[2048]{0:T(1024)S(1)} %copy-done.11, f32[512,4]{0,1:T(4,128)S(1)} %add_rsqrt_fusion, bf16[1,512,2048]{1,2,0:T(8,128)(2,1)S(1)} %copy.55), kind=kLoop, calls=%fused_computation.50 | loop fusion | flops 9437184 | bytes 8404992 | tf_op jit(solution)/shard_map/convert_element_type | solution.py:90
  106.5 260.8 %all-gather.6.cloned.1.call-done = bf16[2048,4096]{1,0:T(8,128)(2,1)} async-done(((bf16[2048,1024]{1,0:T(8,128)(2,1)}), bf16[2048,4096]{1,0:T(8,128)(2,1)}) %all-gather.6.cloned.1.call-update) | async-done | bytes 16777232 | tf_op jit(solution)/shard_map/all_gather | solution.py:128
  367.3 14.6 %convolution_convert_fusion = bf16[512,4096]{1,0:T(8,128)(2,1)} fusion(bf16[512,2048]{0,1:T(8,128)(2,1)} %fusion.21, bf16[2048,4096]{1,0:T(8,128)(2,1)} %all-gather.6.cloned.1.call-done), kind=kOutput, calls=%fused_computation.47 | convolution fusion | flops 8592031744 | bytes 23068672 | tf_op jit(solution)/shard_map/dot_general | solution.py:126
  381.9 10.2 %reduce-scatter.2.cloned.1.call-done = bf16[512,2048]{1,0:T(8,128)(2,1)} async-done(((bf16[512,4096]{1,0:T(8,128)(2,1)}), bf16[512,2048]{1,0:T(8,128)(2,1)}) %reduce-scatter.2.cloned.1.call-update) | async-done | bytes 2097168 | tf_op jit(solution)/shard_map/reduce_scatter | solution.py:131
  (117 shorter events, 6.9 us)
Async XLA Ops:
  6.5 73.6 %all-gather.8.cloned.1.call-start = ((), (), s32[]{:S(2)}) async-start(), calls=%async_computation.3 | async-start | bytes 2621440 | tf_op jit(solution)/shard_map/all_gather | solution.py:16
  8.3 1.2 copy-start.3
  8.3 1.2 copy-start.5
  8.3 3.2 copy-start
  8.4 3.2 copy-start.1
  8.4 3.4 copy-start.12
  17.1 1.6 copy-start.8
  17.1 2.4 copy-start.4
  17.1 2.4 copy-start.6
  18.8 0.6 copy-start.9
  19.5 1.2 copy-start.3
  19.5 1.2 copy-start.5
  19.5 3.2 copy-start
  19.5 3.2 copy-start.1
  19.5 3.4 copy-start.12
  28.3 1.6 copy-start.8
  28.3 2.4 copy-start.4
  28.3 2.4 copy-start.6
  30.0 0.6 copy-start.9
  30.7 1.7 copy-start.7
  30.7 2.0 copy-start.10
  31.6 335.7 %all-gather.6.cloned.1.call-start = ((), (), s32[]{:S(2)}) async-start(), calls=%async_computation.1 | async-start | bytes 20971520 | tf_op jit(solution)/shard_map/all_gather | solution.py:128
  32.3 359.8 %reduce-scatter.2.cloned.1.call-start = ((), (), s32[]{:S(2)}) async-start(), calls=%async_computation.2 | async-start | bytes 6291456 | tf_op jit(solution)/shard_map/reduce_scatter | solution.py:131
  83.1 6.6 %copy-start.2 = (bf16[2,1,256,128]{3,2,1,0:T(8,128)(2,1)S(1)}, bf16[2,1,256,128]{3,2,1,0:T(8,128)(2,1)}, u32[]{:S(2)}) copy-start(bf16[2,1,256,128]{3,2,1,0:T(8,128)(2,1)} %get-tuple-element.478) | copy-start | bytes 393220
  99.9 2.6 copy-start.11
Sparse Core Ops, SparseCore 0:
  31.7 48.4 all-gather.7
  81.7 285.5 all-gather.5
  382.0 10.0 reduce-scatter.1
where the time goes:
time: 399 us
  waiting for transfers between devices  286 us (72%)
  matrix products  30.1 us (8%)
  local copies, waits for them, and re-layouts  28.7 us (7%)
  blocking collectives  26.6 us (7%)
  other arithmetic  13.7 us (3%)
  between operations  13.3 us (3%)
    all_gather x1, waiting for transfers between devices, shards(): lax.all_gather(out_weight, 'seq', axis=1, tiled=True)  261 us
    dot_general x1, matrix products, shards(): jnp.dot(normed, lax.all_gather(out_weight, 'seq', axis=1, tiled=True), pr...  14.6 us
    all_gather x1, waiting for transfers between devices, carried_in(): lax.all_gather(a.astype(kind), axis)  13.9 us
    all_gather x1, blocking collectives, shards(): lax.all_gather(prompt_state.astype(jnp.bfloat16), 'sample', axis=2, tiled...  13.7 us
    all_gather x1, blocking collectives, carried_in(): lax.all_gather(a.astype(kind), axis)  12.9 us
    reduce_scatter x1, waiting for transfers between devices, shards(): lax.psum_scatter(terms.astype(jnp.bfloat16), 'head', scatter_dimension=1,...  10.2 us
  transfers between devices with their start and end apart: 3, of which 3 were waited for; matrix products, arithmetic and copies ran while one was open for 8% of the time, Pallas kernels for 0%

commit v1 on v0

--- a/solution.py
+++ b/solution.py
@@ -125,7 +125,7 @@
     normed = group_norm(gated, norm_gain)
     terms = jnp.dot(
         normed,
-        lax.all_gather(out_weight, "seq", axis=1, tiled=True),
+        jnp.concatenate(lax.all_gather(out_weight, "seq"), axis=1),
         preferred_element_type=jnp.float32,
     )
     mine = lax.psum_scatter(terms.astype(jnp.bfloat16), "head", scatter_dimension=1, tiled=True)

time: 399 us -> 421 us (1.055)
  local copies, waits for them, and re-layouts: 28.7 us -> 57.3 us
  waiting for transfers between devices: 286 us -> 279 us
    reshape x2 -> x4, local copies, waits for them, and re-layouts: 0.01 us -> 28.3 us  [the longest x1 21.8 us: shards(): jnp.concatenate(lax.all_gather(out_weight, 'seq'), axis=1)]
    unnamed x11, local copies, waits for them, and re-layouts: 5.58 us -> 0.54 us
    convert_element_type x1 -> x2, local copies, waits for them, and re-layouts: 3.99 us -> 8.86 us  [shards(): gate_values.reshape(samples * tokens, -1).astype(jnp.float32)]
    all_gather x1, waiting for transfers between devices: 261 us -> 256 us  [shards(): lax.all_gather(out_weight, 'seq')]
  transfers between devices with their start and end apart: 3 -> 3, of which waited for: 3 -> 3; matrix products, arithmetic and copies ran while one was open for 8% -> 10% of each run, Pallas kernels for 0% -> 0%
where the time goes in v1:
time: 421 us; the launch traced here: 420 us
  waiting for transfers between devices  279 us (66%)
  local copies, waits for them, and re-layouts  57.3 us (14%)
  matrix products  29.7 us (7%)
  blocking collectives  26.4 us (6%)
  other arithmetic  13.3 us (3%)
  between operations  13.3 us (3%)
    all_gather x1, waiting for transfers between devices, shards(): lax.all_gather(out_weight, 'seq')  256 us
    reshape x1, local copies, waits for them, and re-layouts, shards(): jnp.concatenate(lax.all_gather(out_weight, 'seq'), axis=1)  21.8 us
    dot_general x1, matrix products, shards(): jnp.dot(normed, jnp.concatenate(lax.all_gather(out_weight, 'seq'), axis=1...  13.9 us
    all_gather x1, blocking collectives, shards(): lax.all_gather(prompt_state.astype(jnp.bfloat16), 'sample', axis=2, tiled...  13.3 us
    all_gather x1, blocking collectives, carried_in(): lax.all_gather(a.astype(kind), axis)  13.1 us
    all_gather x1, waiting for transfers between devices, carried_in(): lax.all_gather(a.astype(kind), axis)  11.9 us
    reduce_scatter x1, waiting for transfers between devices, shards(): lax.psum_scatter(terms.astype(jnp.bfloat16), 'head', scatter_dimension=1,...  10.2 us
    convert_element_type x2, local copies, waits for them, and re-layouts, shards(): gate_values.reshape(samples * tokens, -1).astype(jnp.float32)  8.86 us
  transfers between devices with their start and end apart: 3, of which 3 were waited for; matrix products, arithmetic and copies ran while one was open for 10% of the time, Pallas kernels for 0%

profile of v1, /device:TPU:0, one launch (start us, length us, event | category | flops | bytes accessed | tf_op | source)
XLA Modules:
  0.0 419.8 jit_solution(17606641393341831787)
XLA Ops:
  6.5 0.9 reshape.340
  7.4 0.9 reshape.342
  8.3 22.3 %while.34 = (s32[]{:T(128)}, f32[1,32,64,128]{3,2,1,0:T(8,128)S(1)}, f32[1,32]{1,0:T(1,128)S(1)}, f32[2,1,256,32,64]{2,4,3,1,0:T(8,128)}, f32[2,1,256,32]{2,0,3,...) while((s32[]{:T(128)}, ...), condition=%wide.region_3.4_spmd.clone, body=%wide.region_0.3_spmd.clone.sunk | while | flops 435765440 | bytes 33923384 | solution.py:76
  8.5 0.6 reduce-window.14
  9.6 1.3 constant_dynamic-slice_fusion.7
  10.9 0.5 copy.95
  11.8 3.7 fusion.43
  17.1 1.0 bitcast_dynamic-update-slice_fusion.2
  18.9 0.6 copy-done.10
  19.6 0.6 reduce-window.14
  20.7 1.3 constant_dynamic-slice_fusion.7
  23.0 3.7 fusion.43
  28.3 1.0 bitcast_dynamic-update-slice_fusion.2
  30.0 0.6 copy-done.10
  30.6 0.9 convert_element_type.153
  31.6 0.7 all-gather.9.cloned.1.call-update
  33.0 3.0 copy.58
  35.9 5.9 %reshape.356 = f32[2,256,32,64]{1,0,3,2:T(2,128)} reshape(f32[1,512,2048]{1,2,0:T(8,128)} %copy.58) | data formatting | bytes 8388608 | tf_op jit(solution)/shard_map/convert_element_type | solution.py:124
  41.9 13.1 %all-gather.3 = bf16[4,1,32]{2,1,0:T(2,128)(2,1)S(1)} all-gather(bf16[1,1,32]{2,1,0:T(2,128)(2,1)S(1)} %convert_bitcast_fusion.1), channel_id=2, replica_groups=mesh['sample'=4,'seq'=4,'head'=2] {'seq'}, dimensions={0}, use_global_device_ids=true | all-gather | bytes 320 | tf_op jit(solution)/shard_map/all_gather | solution.py:16
  55.0 13.3 %all_gather.25 = bf16[32,64,128]{1,0,2:T(8,128)(2,1)} all-gather(bf16[32,64,32]{1,0,2:T(8,128)(2,1)S(1)} %copy.76), channel_id=1, replica_groups=mesh['sample'=4,'seq'=4,'head'=2] {'sample'}, dimensions={2}, use_global_device_ids=true | all-gather | bytes 655360 | tf_op jit(solution)/shard_map/all_gather | solution.py:105
  68.3 11.9 %all-gather.7.cloned.1.call-done = bf16[4,32,64,128]{3,2,1,0:T(8,128)(2,1)} async-done(((bf16[1,32,64,128]{3,2,1,0:T(8,128)(2,1)}), bf16[4,32,64,128]{3,2,1,0:T(8,128)(2,1)}) %all-gather.7.cloned.1.call-update) | async-done | bytes 2097168 | tf_op jit(solution)/shard_map/all_gather | solution.py:16
  80.3 1.8 copy.55
  82.1 3.0 fusion.21
  85.1 2.7 copy.56
  87.8 7.0 %multiply_reduce_fusion = (f32[2,256,32]{1,2,0:T(8,128)S(1)}, f32[2,256,32,64]{1,3,2,0:T(8,128)S(1)}) fusion(f32[2,256,32,64]{1,0,3,2:T(2,128)} %reshape.356, bf16[2,256,128,1]{2,1,3,0:T(8,128)(2,1)S(1)} %bitcast.210, f32[2,1,32,64,128]{4,3,2,1,0:T(8,128)} %get-tuple-element.113, f32[32,64,128]{2,1,0:T(8,128)S(1)} %copy.56, f32[2,32]{1,0:T(2,128)S(1)} %bitcast.213, ...), kind=kOutput, calls=%fused_computation.51 | convolution fusion | flops 279429120 | bytes 15991040 | tf_op jit(solution)/shard_map/sktn,skhpn->skthp/dot_general | solution.py:120
  94.8 5.2 %copy.57 = f32[2,256,32,64]{1,0,3,2:T(2,128)} copy(f32[2,256,32,64]{1,3,2,0:T(8,128)S(1)} %get-tuple-element.267) | data formatting | bytes 8388608 | tf_op jit(solution)/shard_map/add | solution.py:123
  100.0 6.5 %reshape.346 = f32[512,4,512]{0,2,1:T(8,128)} reshape(f32[2,256,32,64]{1,0,3,2:T(2,128)} %copy.57) | data formatting | bytes 8388608 | tf_op jit(solution)/shard_map/reshape | solution.py:123
  106.7 4.3 %multiply_convert_fusion.8 = bf16[512,4,512]{0,2,1:T(8,128)(2,1)S(1)} fusion(f32[512,4,512]{0,2,1:T(8,128)} %reshape.346, f32[512,4,512]{0,2,1:T(8,128)} %bitcast.194, f32[4,512]{1,0:T(4,128)S(1)} %mul.210, f32[512,4]{0,1:T(4,128)S(1)} %add_rsqrt_fusion), kind=kLoop, calls=%fused_computation.50 | loop fusion | flops 8388608 | bytes 10502144 | tf_op jit(solution)/shard_map/convert_element_type | solution.py:90
  110.9 256.3 %all-gather.9.cloned.1.call-done = bf16[8192,1024]{1,0:T(8,128)(2,1)} async-done(((bf16[2048,1024]{1,0:T(8,128)(2,1)}), bf16[8192,1024]{1,0:T(8,128)(2,1)}) %all-gather.9.cloned.1.call-update) | async-done | bytes 16777232 | tf_op jit(solution)/shard_map/all_gather | solution.py:128
  367.3 21.8 %copy.63 = bf16[2048,4,1024]{0,2,1:T(8,128)(2,1)} copy(bf16[2048,4,1024]{2,0,1:T(8,128)(2,1)} %bitcast.195) | data formatting | bytes 33554432 | tf_op jit(solution)/shard_map/reshape | solution.py:128
  389.1 13.9 %convolution_convert_fusion = bf16[512,4096]{1,0:T(8,128)(2,1)} fusion(bf16[512,2048]{0,1:T(8,128)(2,1)S(1)} %bitcast.208, bf16[2048,4096]{0,1:T(8,128)(2,1)} %bitcast.196), kind=kOutput, calls=%fused_computation.47 | convolution fusion | flops 8592031744 | bytes 23068672 | tf_op jit(solution)/shard_map/dot_general | solution.py:126
  403.0 10.2 %reduce-scatter.2.cloned.1.call-done = bf16[512,2048]{1,0:T(8,128)(2,1)} async-done(((bf16[512,4096]{1,0:T(8,128)(2,1)}), bf16[512,2048]{1,0:T(8,128)(2,1)}) %reduce-scatter.2.cloned.1.call-update) | async-done | bytes 2097168 | tf_op jit(solution)/shard_map/reduce_scatter | solution.py:131
  (121 shorter events, 7.6 us)
Async XLA Ops:
  6.5 73.6 %all-gather.7.cloned.1.call-start = ((), (), s32[]{:S(2)}) async-start(), calls=%async_computation.2 | async-start | bytes 2621440 | tf_op jit(solution)/shard_map/all_gather | solution.py:16
  8.3 1.2 copy-start.4
  8.3 1.2 copy-start.6
  8.3 3.2 copy-start
  8.4 3.2 copy-start.2
  8.4 3.4 copy-start.13
  17.1 1.6 copy-start.9
  17.1 2.4 copy-start.5
  17.1 2.4 copy-start.7
  18.8 0.6 copy-start.10
  19.5 1.2 copy-start.4
  19.5 1.2 copy-start.6
  19.5 3.2 copy-start
  19.5 3.2 copy-start.2
  19.5 3.4 copy-start.13
  28.2 1.6 copy-start.9
  28.2 2.4 copy-start.5
  28.2 2.4 copy-start.7
  30.0 0.6 copy-start.10
  30.6 2.2 copy-start.11
  30.6 2.3 copy-start.1
  31.5 1.0 copy-start.8
  31.6 335.7 %all-gather.9.cloned.1.call-start = ((), (), s32[]{:S(2)}) async-start(), calls=%async_computation.3 | async-start | bytes 20971520 | tf_op jit(solution)/shard_map/all_gather | solution.py:128
  32.3 380.9 %reduce-scatter.2.cloned.1.call-start = ((), (), s32[]{:S(2)}) async-start(), calls=%async_computation.1 | async-start | bytes 6291456 | tf_op jit(solution)/shard_map/reduce_scatter | solution.py:131
  35.9 5.9 %copy-start.12 = (f32[2048]{0:T(1024)S(1)}, f32[2048]{0:T(1024)}, u32[]{:S(2)}) copy-start(f32[2048]{0:T(1024)} %param.21) | copy-start | bytes 24580
  82.1 5.7 %copy-start.3 = (bf16[2,1,256,128]{3,2,1,0:T(8,128)(2,1)S(1)}, bf16[2,1,256,128]{3,2,1,0:T(8,128)(2,1)}, u32[]{:S(2)}) copy-start(bf16[2,1,256,128]{3,2,1,0:T(8,128)(2,1)} %get-tuple-element.479) | copy-start | bytes 393220
Sparse Core Ops, SparseCore 0:
  31.7 48.4 all-gather.6
  81.7 285.5 all-gather.8
  403.1 10.0 reduce-scatter.1
